TPU v7x, 512 devices: a whole 4x8x8 slice. The times are simulated.
512 devices in a mesh: req: 64 (over x, y, core), head: 8 (over z).
Axes of the slice: x: 4, y: 8, z: 8, core: 2. Of those that a mesh axis runs over, the one named last changes fastest.
Arguments:
- hidden: bfloat16 [512, 4096], P(None, 'req'), may hold values from -16 to 16
- query_key_value_weight: bfloat16 [4096, 8, 768], P('req', 'head'), may hold values from -0.1875 to 0.1875
- output_weight: bfloat16 [4096, 4096], P('head', 'req'), may hold values from -0.375 to 0.375
- kv_pool: bfloat16 [4096, 8, 128, 256], P('req', 'head'), may hold values from -68 to 68
- lengths: int32 [512], P('req'), may hold values from 513 to 2048, as said below
- page_table: int32 [512, 16], P('req'), may hold values from 0 to 127, as said below
- send_slots: int32 [4096], P('req'), may hold values from 0 to 63, as said below
Outputs:
- attn_out: bfloat16 [512, 4096], P('head', 'req')
Inputs may be any that keep to these rules, and one draw needn't show every extreme that they name: `page_table`: A request's live positions name distinct slots of its group's store, and every other entry is 0. Slots below 64 are the group's own pool rows; slot 64 + s is the page that group s sends to it. Every group uses exactly 32 of the 64 pages sent to it, never for a long request. `send_slots`: every group sends one page to every group; rows whose page the receiver does not use name an arbitrary slot. In 16 of the groups one request is long (more than (15) * 128 tokens); all others hold at most 768 tokens. The new token sits at position lengths[r].
All inputs are finite; a program needn't handle non-finite values.
Results may differ from a plain program's by a relative error of at most 0.018.
Values may be sent and summed in bfloat16 or wider, within the bound.
A program may use at most 64 MiB of HBM per device.

v0:
```python
import jax
import jax.numpy as jnp
from jax import lax
from jax.sharding import PartitionSpec as P

ROPE_BASE = 500000.0
NEG_FILL = -1e30


def rotate(vectors, angles):
    half_width = vectors.shape[-1] // 2
    first_half = vectors[..., :half_width]
    second_half = vectors[..., half_width:]
    cosine = jnp.cos(angles)
    sine_part = jnp.sin(angles)
    return jnp.concatenate(
        [
            first_half * cosine - second_half * sine_part,
            second_half * cosine + first_half * sine_part,
        ],
        axis=-1,
    )


def rope_angles(lengths, width):
    exponent = jnp.arange(width // 2, dtype=jnp.float32) * (2.0 / width)
    inverse = 1.0 / ROPE_BASE**exponent
    return lengths.astype(jnp.float32)[:, None] * inverse[None, :]


def split_projection(projected_rows, lengths):
    angles = rope_angles(lengths, projected_rows.shape[-1])
    queries = rotate(projected_rows[:, :, :-2], angles[:, None, None, :]).astype(jnp.bfloat16)
    new_keys = rotate(projected_rows[:, :, -2], angles[:, None, :]).astype(jnp.bfloat16)
    new_values = projected_rows[:, :, -1].astype(jnp.bfloat16)
    return (queries, new_keys, new_values)


def page_stats(queries, pages, valid_tokens, score_scale):
    head_dim = pages.shape[-1] // 2
    scores = (
        jnp.einsum(
            "nhqd,nhtd->nhqt", queries, pages[..., :head_dim], preferred_element_type=jnp.float32
        )
        * score_scale
    )
    token_mask = jnp.arange(pages.shape[2])[None, None, None, :] < valid_tokens[:, None, None, None]
    masked = jnp.where(token_mask, scores, NEG_FILL)
    top_score = jnp.max(masked, axis=-1)
    weights = jnp.where(token_mask, jnp.exp(scores - top_score[..., None]), 0.0)
    weight_sum = jnp.sum(weights, axis=-1)
    weighted_values = jnp.einsum(
        "nhqt,nhtd->nhqd",
        weights.astype(jnp.bfloat16),
        pages[..., head_dim:],
        preferred_element_type=jnp.float32,
    )
    return (top_score, weight_sum, weighted_values)


def shards(hidden, query_key_value_weight, output_weight, kv_pool, lengths, page_table, send_slots):
    groups = lax.axis_size("req")
    local_count = lengths.shape[0]
    head_count = query_key_value_weight.shape[1]
    pool_slots = kv_pool.shape[0]
    page_len = kv_pool.shape[2]
    head_dim = kv_pool.shape[3] // 2
    per_head = query_key_value_weight.shape[2] // head_dim
    flat_weight = query_key_value_weight.reshape(
        query_key_value_weight.shape[0], head_count * per_head * head_dim
    )
    projected_rows = lax.psum_scatter(
        jnp.dot(hidden, flat_weight, preferred_element_type=jnp.float32),
        "req",
        scatter_dimension=0,
        tiled=True,
    )
    projected_rows = projected_rows.reshape(local_count, head_count, per_head, head_dim)
    queries, new_keys, new_values = split_projection(projected_rows, lengths)
    score_scale = head_dim ** (-0.5)
    self_scores = (
        jnp.sum(queries.astype(jnp.float32) * new_keys.astype(jnp.float32)[:, :, None, :], axis=-1)
        * score_scale
    )
    total_slots = pool_slots + groups
    places = jnp.arange(page_table.shape[1], dtype=jnp.int32)
    is_live = places[None, :] * page_len < lengths[:, None]
    tokens_in = jnp.clip(lengths[:, None] - places[None, :] * page_len, 0, page_len)
    table_hits = (
        page_table[:, :, None] == jnp.arange(total_slots, dtype=jnp.int32)[None, None, :]
    ) & is_live[:, :, None]
    owner_map = jnp.any(table_hits, axis=1).T
    valid_tokens = jnp.sum(jnp.where(table_hits, tokens_in[:, :, None], 0), axis=(0, 1))
    owner_index = jnp.sum(
        jnp.where(owner_map, jnp.arange(local_count, dtype=jnp.int32)[None, :], 0), axis=1
    )
    slot_queries = jnp.einsum(
        "nr,rhqd->nhqd", owner_map.astype(jnp.bfloat16), queries, preferred_element_type=jnp.float32
    ).astype(jnp.bfloat16)
    outgoing = kv_pool[send_slots]
    arrived = lax.all_to_all(outgoing, "req", split_axis=0, concat_axis=0, tiled=True)
    page_store = jnp.concatenate([kv_pool, arrived], axis=0)
    page_max, page_sum, page_acc = page_stats(slot_queries, page_store, valid_tokens, score_scale)
    owned_max = jnp.max(jnp.where(owner_map[:, :, None, None], page_max[:, None], NEG_FILL), axis=0)
    top_score = jnp.maximum(owned_max, self_scores)
    factors = jnp.exp(page_max - top_score[owner_index])
    owner_float = owner_map.astype(jnp.float32)
    self_weight = jnp.exp(self_scores - top_score)
    total_weight_sum = (
        jnp.einsum("nr,nhq->rhq", owner_float, factors * page_sum, precision=lax.Precision.HIGHEST)
        + self_weight
    )
    weighted_values = jnp.einsum(
        "nr,nhqd->rhqd", owner_float, factors[..., None] * page_acc, precision=lax.Precision.HIGHEST
    )
    weighted_values = (
        weighted_values + self_weight[..., None] * new_values.astype(jnp.float32)[:, :, None, :]
    )
    output_per_head = (
        (weighted_values / total_weight_sum[..., None])
        .astype(jnp.bfloat16)
        .reshape(local_count, head_count * (per_head - 2) * head_dim)
    )
    partial_out = jnp.dot(
        lax.all_gather(output_per_head, "req", axis=0, tiled=True),
        output_weight,
        preferred_element_type=jnp.float32,
    )
    return lax.psum_scatter(
        partial_out.astype(jnp.bfloat16), "head", scatter_dimension=0, tiled=True
    )


def solution(mesh):
    return jax.shard_map(
        shards,
        mesh=mesh,
        in_specs=(
            P(None, "req"),
            P("req", "head", None),
            P("head", "req"),
            P("req", "head", None, None),
            P("req"),
            P("req", None),
            P("req"),
        ),
        out_specs=P("head", "req"),
        check_vma=False,
    )
```

profile of v0, /device:TPU:2, one launch (start us, length us, event | category | flops | bytes accessed | tf_op | source)
XLA Modules:
  0.0 291.1 jit_solution(14235447509010207527)
XLA Ops:
  6.5 0.0 copy-start
  6.5 0.7 compare_select_fusion.1
  7.2 5.0 %gather_fusion = bf16[64,128,256]{2,1,0:T(8,128)(2,1)} fusion(bf16[64,128,256]{2,1,0:T(8,128)(2,1)} %bitcast.50, s32[1024]{0:T(1024)S(1)} %pad_clamp_fusion.1), kind=kCustom, calls=%fused_computation | custom fusion | bytes 8388864 | tf_op jit(solution)/shard_map/gather | solution.py:100
  12.2 0.0 copy-start.2
  12.2 0.0 copy-start.4
  12.2 0.0 copy-start.3
  12.2 11.1 %all-to-all-start = ((bf16[64,1,128,256]{3,2,1,0:T(8,128)(2,1)}), bf16[64,1,128,256]{3,2,1,0:T(8,128)(2,1)}, u32[]{:S(2)}, u32[]{:S(2)}) async-start(bf16[64,1,128,256]{3,2,1,0:T(8,128)(2,1)} %bitcast.53), calls=%async_computation.1 | async-start | bytes 8388608 | tf_op jit(solution)/shard_map/all_to_all | solution.py:101
  23.4 0.0 reduce-scatter.3.cloned.1.call-start
  23.4 0.0 copy-done
  23.4 0.0 copy-done.2
  23.4 1.6 fusion.25
  25.0 0.0 reduce-scatter.3.cloned.1.call-update
  25.1 0.0 reduce-scatter.5.cloned.1.call-start
  25.1 0.0 copy-done.4
  25.2 0.1 broadcast_compare_fusion
  25.2 0.0 copy-done.3
  25.2 0.1 fusion.29
  25.4 0.1 subtract_clamp_fusion
  25.5 0.1 select_reduce_fusion.1
  25.6 0.1 multiply_cosine_fusion.1
  25.7 0.1 iota_compare_fusion
  25.8 155.3 %reduce-scatter.3.cloned.1.call-done = f32[8,768]{1,0:T(8,128)} async-done(((f32[512,768]{1,0:T(8,128)}), f32[8,768]{1,0:T(8,128)}) %reduce-scatter.3.cloned.1.call-update) | async-done | bytes 24592 | tf_op jit(solution)/shard_map/reduce_scatter | solution.py:72
  181.1 0.7 slice_bitcast_fusion
  181.8 0.1 fusion.46
  181.9 0.1 maximum_convert_fusion
  182.0 0.9 subtract_convert_fusion
  182.9 0.2 multiply_reduce_fusion
  183.0 0.7 fusion.44
  183.7 0.3 convolution_convert_fusion.1
  184.0 0.0 all-to-all-done
  184.0 4.6 %select_reduce_fusion = (f32[128,4]{1,0:T(8,128)S(1)}, f32[128,4,128]{2,1,0:T(4,128)S(1)}) fusion(pred[128,128]{1,0:T(8,128)(4,1)S(1)} %iota_compare_fusion, bf16[64,1,128,256]{3,2,0,1:T(8,128)(2,1)} %bitcast.51, bf16[64,1,128,256]{3,2,0,1:T(8,128)(2,1)} %bitcast.8, bf16[128,4,128]{2,0,1:T(8,128)(2,1)S(1)} %convolution_convert_fusion.1), kind=kOutput, calls=%fused_computation.22 | convolution fusion | flops 19070464 | bytes 8800256 | tf_op jit(solution)/shard_map/nhqd,nhtd->nhqt/dot_general | solution.py:42
  188.6 0.1 copy.20
  188.6 0.1 select_reduce_fusion.2
  188.8 0.1 copy.21
  188.8 0.7 gather_fusion.1
  189.5 0.4 fusion.18
  189.9 0.0 copy-start.1
  189.9 3.5 %fusion.11 = f32[128,4,128]{2,1,0:T(4,128)S(1)} fusion(bf16[64,1,128,256]{3,2,0,1:T(8,128)(2,1)} %bitcast.8, bf16[64,1,128,256]{3,2,0,1:T(8,128)(2,1)} %bitcast.52, f32[128,4,128]{2,1,0:T(4,128)S(1)} %get-tuple-element.14, f32[128,4]{1,0:T(8,128)S(1)} %get-tuple-element.13, f32[128,4]{1,0:T(8,128)S(1)} %subtract_exponential_fusion, ...), kind=kOutput, calls=%fused_computation.12 | convolution fusion | flops 25427968 | bytes 8933376 | tf_op jit(solution)/shard_map/nhqt,nhtd->nhqd/dot_general | solution.py:52
  193.4 0.2 convolution_add_fusion.1
  193.6 0.2 fusion.16
  193.9 48.6 %all_gather.3 = bf16[512,512]{1,0:T(8,128)(2,1)S(1)} all-gather(bf16[8,512]{1,0:T(8,128)(2,1)S(1)} %fusion.16), channel_id=1, replica_groups=mesh['req'=64,'head'=8] {'req'}, dimensions={0}, use_global_device_ids=true | all-gather | bytes 532480 | tf_op jit(solution)/shard_map/all_gather | solution.py:125
  242.5 0.0 copy-done.1
  242.5 0.9 convolution_convert_fusion
  243.4 0.0 reduce-scatter.5.cloned.1.call-update
  243.4 40.8 %reduce-scatter.5.cloned.1.call-done = bf16[64,64]{1,0:T(8,128)(2,1)} async-done(((bf16[512,64]{1,0:T(8,128)(2,1)}), bf16[64,64]{1,0:T(8,128)(2,1)}) %reduce-scatter.5.cloned.1.call-update) | async-done | bytes 8208 | tf_op jit(solution)/shard_map/reduce_scatter | solution.py:129
  (9 shorter events, 0.1 us)
Async XLA Ops:
  6.5 16.9 %copy-start = (bf16[64,1,768]{2,0,1:T(8,128)(2,1)S(1)}, bf16[64,1,768]{2,0,1:T(8,128)(2,1)}, u32[]{:S(2)}) copy-start(bf16[64,1,768]{2,0,1:T(8,128)(2,1)} %param.8) | copy-start | bytes 294916
  12.2 11.2 %copy-start.2 = (bf16[512,64]{0,1:T(8,128)(2,1)S(1)}, bf16[512,64]{0,1:T(8,128)(2,1)}, u32[]{:S(2)}) copy-start(bf16[512,64]{0,1:T(8,128)(2,1)} %param.7) | copy-start | bytes 196612
  12.2 12.9 %copy-start.4 = (s32[8]{0:T(128)S(1)}, s32[8]{0:T(128)}, u32[]{:S(2)}) copy-start(s32[8]{0:T(128)} %param.11) | copy-start | bytes 100
  12.2 13.0 %copy-start.3 = (s32[8,16]{1,0:T(8,128)S(1)}, s32[8,16]{1,0:T(8,128)}, u32[]{:S(2)}) copy-start(s32[8,16]{1,0:T(8,128)} %param.12) | copy-start | bytes 1540
  12.2 171.8 %all-to-all-start = ((bf16[64,1,128,256]{3,2,1,0:T(8,128)(2,1)}), bf16[64,1,128,256]{3,2,1,0:T(8,128)(2,1)}, u32[]{:S(2)}, u32[]{:S(2)}) async-start(bf16[64,1,128,256]{3,2,1,0:T(8,128)(2,1)} %bitcast.53), calls=%async_computation.1 | async-start | bytes 8388608 | tf_op jit(solution)/shard_map/all_to_all | solution.py:101
  23.4 157.7 %reduce-scatter.3.cloned.1.call-start = ((), (), s32[]{:S(2)}) async-start(), calls=%async_computation.3 | async-start | bytes 1597440 | tf_op jit(solution)/shard_map/reduce_scatter | solution.py:72
  25.1 259.2 %reduce-scatter.5.cloned.1.call-start = ((), (), s32[]{:S(2)}) async-start(), calls=%async_computation.4 | async-start | bytes 147456 | tf_op jit(solution)/shard_map/reduce_scatter | solution.py:129
  189.9 52.6 %copy-start.1 = (bf16[512,64]{0,1:T(8,128)(2,1)S(1)}, bf16[512,64]{0,1:T(8,128)(2,1)}, u32[]{:S(2)}) copy-start(bf16[512,64]{0,1:T(8,128)(2,1)} %param.9) | copy-start | bytes 196612
Sparse Core Ops, SparseCore 0:
  28.8 152.2 reduce-scatter.2
  243.6 40.6 reduce-scatter.4
where the time goes:
time: 292 us; the launch traced here: 291 us
  waiting for transfers between devices  196 us (67%)
  blocking collectives  48.6 us (17%)
  between operations  13.5 us (5%)
  matrix products  11.3 us (4%)
  starting transfers between devices  11.2 us (4%)
  local copies, waits for them, and re-layouts  6.47 us (2%)
  other arithmetic  3.76 us (1%)
    reduce_scatter x1, waiting for transfers between devices, shards(): lax.psum_scatter(jnp.dot(hidden, flat_weight, preferred_element_type=jnp....  155 us
    all_gather x1, blocking collectives, shards(): lax.all_gather(output_per_head, 'req', axis=0, tiled=True)  48.6 us
    reduce_scatter x1, waiting for transfers between devices, shards(): lax.psum_scatter(partial_out.astype(jnp.bfloat16), 'head', scatter_dimens...  40.8 us
    all_to_all x1, starting transfers between devices, shards(): lax.all_to_all(outgoing, 'req', split_axis=0, concat_axis=0, tiled=True)  11.1 us
  transfers between devices with their start and end apart: 3, of which 2 were waited for; matrix products, arithmetic and copies ran while one was open for 2% of the time, Pallas kernels for 0%

commit v1 on v0

--- a/solution.py
+++ b/solution.py
@@ -5,6 +5,14 @@
 
 ROPE_BASE = 500000.0
 NEG_FILL = -1e30
+
+
+def gather_by_exchange(value, axis, dim):
+    length = lax.axis_size(axis)
+    repeats = [length if d == dim else 1 for d in range(value.ndim)]
+    return lax.all_to_all(
+        jnp.tile(value, repeats), axis, split_axis=dim, concat_axis=dim, tiled=True
+    )
 
 
 def rotate(vectors, angles):
@@ -122,7 +130,7 @@
         .reshape(local_count, head_count * (per_head - 2) * head_dim)
     )
     partial_out = jnp.dot(
-        lax.all_gather(output_per_head, "req", axis=0, tiled=True),
+        gather_by_exchange(output_per_head, "req", 0),
         output_weight,
         preferred_element_type=jnp.float32,
     )

time: 292 us -> 266 us (0.911)
  blocking collectives: 48.6 us -> 25.1 us
    all_gather x1 -> x0, blocking collectives: 48.6 us -> none  [shards(): lax.all_gather(output_per_head, 'req', axis=0, tiled=True)]
    all_to_all x0 -> x1, blocking collectives: none -> 25.1 us  [gather_by_exchange(): lax.all_to_all(jnp.tile(value, repeats), axis, split_axis=dim, concat_axi...]
where the time goes in v1:
time: 266 us; the launch traced here: 265 us
  waiting for transfers between devices  194 us (73%)
  blocking collectives  25.1 us (9%)
  between operations  13.5 us (5%)
  matrix products  11.3 us (4%)
  starting transfers between devices  11.2 us (4%)
  local copies, waits for them, and re-layouts  6.51 us (2%)
  other arithmetic  3.76 us (1%)
    reduce_scatter x1, waiting for transfers between devices, shards(): lax.psum_scatter(jnp.dot(hidden, flat_weight, preferred_element_type=jnp....  155 us
    reduce_scatter x1, waiting for transfers between devices, shards(): lax.psum_scatter(partial_out.astype(jnp.bfloat16), 'head', scatter_dimens...  38.5 us
    all_to_all x1, blocking collectives, gather_by_exchange(): lax.all_to_all(jnp.tile(value, repeats), axis, split_axis=dim, concat_axi...  25.1 us
    all_to_all x1, starting transfers between devices, shards(): lax.all_to_all(outgoing, 'req', split_axis=0, concat_axis=0, tiled=True)  11.1 us
  transfers between devices with their start and end apart: 3, of which 2 were waited for; matrix products, arithmetic and copies ran while one was open for 2% of the time, Pallas kernels for 0%

profile of v1, /device:TPU:2, one launch (start us, length us, event | category | flops | bytes accessed | tf_op | source)
XLA Modules:
  0.0 265.3 jit_solution(14369854928838752136)
XLA Ops:
  6.5 0.0 copy-start
  6.5 0.7 compare_select_fusion.1
  7.2 5.0 %gather_fusion = bf16[64,128,256]{2,1,0:T(8,128)(2,1)} fusion(bf16[64,128,256]{2,1,0:T(8,128)(2,1)} %bitcast.52, s32[1024]{0:T(1024)S(1)} %pad_clamp_fusion.1), kind=kCustom, calls=%fused_computation | custom fusion | bytes 8388864 | tf_op jit(solution)/shard_map/gather | solution.py:108
  12.2 0.0 copy-start.2
  12.2 0.0 copy-start.4
  12.2 0.0 copy-start.3
  12.2 11.1 %all-to-all-start = ((bf16[64,1,128,256]{3,2,1,0:T(8,128)(2,1)}), bf16[64,1,128,256]{3,2,1,0:T(8,128)(2,1)}, u32[]{:S(2)}, u32[]{:S(2)}) async-start(bf16[64,1,128,256]{3,2,1,0:T(8,128)(2,1)} %bitcast.55), calls=%async_computation.1 | async-start | bytes 8388608 | tf_op jit(solution)/shard_map/all_to_all | solution.py:109
  23.4 0.0 reduce-scatter.3.cloned.1.call-start
  23.4 0.0 copy-done
  23.4 0.0 copy-done.2
  23.4 1.6 fusion.26
  25.0 0.0 reduce-scatter.3.cloned.1.call-update
  25.1 0.0 reduce-scatter.5.cloned.1.call-start
  25.1 0.0 copy-done.4
  25.2 0.1 broadcast_compare_fusion
  25.2 0.0 copy-done.3
  25.2 0.1 fusion.30
  25.4 0.1 subtract_clamp_fusion
  25.5 0.1 select_reduce_fusion.1
  25.6 0.1 multiply_cosine_fusion.1
  25.7 0.1 iota_compare_fusion
  25.8 155.3 %reduce-scatter.3.cloned.1.call-done = f32[8,768]{1,0:T(8,128)} async-done(((f32[512,768]{1,0:T(8,128)}), f32[8,768]{1,0:T(8,128)}) %reduce-scatter.3.cloned.1.call-update) | async-done | bytes 24592 | tf_op jit(solution)/shard_map/reduce_scatter | solution.py:80
  181.1 0.7 slice_bitcast_fusion
  181.8 0.1 fusion.47
  181.9 0.1 maximum_convert_fusion
  182.0 0.9 subtract_convert_fusion
  182.9 0.2 multiply_reduce_fusion
  183.0 0.7 fusion.45
  183.7 0.3 convolution_convert_fusion.1
  184.0 0.0 all-to-all-done
  184.0 4.6 %select_reduce_fusion = (f32[128,4]{1,0:T(8,128)S(1)}, f32[128,4,128]{2,1,0:T(4,128)S(1)}) fusion(pred[128,128]{1,0:T(8,128)(4,1)S(1)} %iota_compare_fusion, bf16[64,1,128,256]{3,2,0,1:T(8,128)(2,1)} %bitcast.53, bf16[64,1,128,256]{3,2,0,1:T(8,128)(2,1)} %bitcast.8, bf16[128,4,128]{2,0,1:T(8,128)(2,1)S(1)} %convolution_convert_fusion.1), kind=kOutput, calls=%fused_computation.23 | convolution fusion | flops 19070464 | bytes 8800256 | tf_op jit(solution)/shard_map/nhqd,nhtd->nhqt/dot_general | solution.py:50
  188.6 0.1 copy.20
  188.6 0.1 select_reduce_fusion.2
  188.8 0.1 copy.21
  188.8 0.7 gather_fusion.1
  189.5 0.4 fusion.19
  189.9 0.0 copy-start.1
  189.9 3.5 %fusion.11 = f32[128,4,128]{2,1,0:T(4,128)S(1)} fusion(bf16[64,1,128,256]{3,2,0,1:T(8,128)(2,1)} %bitcast.8, bf16[64,1,128,256]{3,2,0,1:T(8,128)(2,1)} %bitcast.54, f32[128,4,128]{2,1,0:T(4,128)S(1)} %get-tuple-element.14, f32[128,4]{1,0:T(8,128)S(1)} %get-tuple-element.13, f32[128,4]{1,0:T(8,128)S(1)} %subtract_exponential_fusion, ...), kind=kOutput, calls=%fused_computation.12 | convolution fusion | flops 25427968 | bytes 8933376 | tf_op jit(solution)/shard_map/nhqt,nhtd->nhqd/dot_general | solution.py:60
  193.4 0.2 convolution_add_fusion.1
  193.6 0.2 fusion.16
  193.9 25.1 %all_to_all.14 = bf16[64,8,512]{2,1,0:T(8,128)(2,1)S(1)} all-to-all(bf16[64,8,512]{2,1,0:T(8,128)(2,1)S(1)} %tile.9), channel_id=1, replica_groups=mesh['req'=64,'head'=8] {'req'}, dimensions={0} | all-to-all | bytes 1048576 | tf_op jit(solution)/shard_map/all_to_all | solution.py:13
  219.0 0.0 copy-done.1
  219.0 0.9 convolution_convert_fusion
  219.9 0.0 reduce-scatter.5.cloned.1.call-update
  219.9 38.5 %reduce-scatter.5.cloned.1.call-done = bf16[64,64]{1,0:T(8,128)(2,1)} async-done(((bf16[512,64]{1,0:T(8,128)(2,1)}), bf16[64,64]{1,0:T(8,128)(2,1)}) %reduce-scatter.5.cloned.1.call-update) | async-done | bytes 8208 | tf_op jit(solution)/shard_map/reduce_scatter | solution.py:137
  (10 shorter events, 0.1 us)
Async XLA Ops:
  6.5 16.9 %copy-start = (bf16[64,1,768]{2,0,1:T(8,128)(2,1)S(1)}, bf16[64,1,768]{2,0,1:T(8,128)(2,1)}, u32[]{:S(2)}) copy-start(bf16[64,1,768]{2,0,1:T(8,128)(2,1)} %param.8) | copy-start | bytes 294916
  12.2 11.2 %copy-start.2 = (bf16[512,64]{0,1:T(8,128)(2,1)S(1)}, bf16[512,64]{0,1:T(8,128)(2,1)}, u32[]{:S(2)}) copy-start(bf16[512,64]{0,1:T(8,128)(2,1)} %param.7) | copy-start | bytes 196612
  12.2 12.9 %copy-start.4 = (s32[8]{0:T(128)S(1)}, s32[8]{0:T(128)}, u32[]{:S(2)}) copy-start(s32[8]{0:T(128)} %param.11) | copy-start | bytes 100
  12.2 13.0 %copy-start.3 = (s32[8,16]{1,0:T(8,128)S(1)}, s32[8,16]{1,0:T(8,128)}, u32[]{:S(2)}) copy-start(s32[8,16]{1,0:T(8,128)} %param.12) | copy-start | bytes 1540
  12.2 171.8 %all-to-all-start = ((bf16[64,1,128,256]{3,2,1,0:T(8,128)(2,1)}), bf16[64,1,128,256]{3,2,1,0:T(8,128)(2,1)}, u32[]{:S(2)}, u32[]{:S(2)}) async-start(bf16[64,1,128,256]{3,2,1,0:T(8,128)(2,1)} %bitcast.55), calls=%async_computation.1 | async-start | bytes 8388608 | tf_op jit(solution)/shard_map/all_to_all | solution.py:109
  23.4 157.7 %reduce-scatter.3.cloned.1.call-start = ((), (), s32[]{:S(2)}) async-start(), calls=%async_computation.4 | async-start | bytes 1597440 | tf_op jit(solution)/shard_map/reduce_scatter | solution.py:80
  25.1 233.4 %reduce-scatter.5.cloned.1.call-start = ((), (), s32[]{:S(2)}) async-start(), calls=%async_computation.5 | async-start | bytes 147456 | tf_op jit(solution)/shard_map/reduce_scatter | solution.py:137
  189.9 29.1 %copy-start.1 = (bf16[512,64]{0,1:T(8,128)(2,1)S(1)}, bf16[512,64]{0,1:T(8,128)(2,1)}, u32[]{:S(2)}) copy-start(bf16[512,64]{0,1:T(8,128)(2,1)} %param.9) | copy-start | bytes 196612
Sparse Core Ops, SparseCore 0:
  28.8 152.2 reduce-scatter.2
  220.1 38.3 reduce-scatter.4
